TPU v7x, 128 devices: a whole 4x4x4 slice. The times are simulated.
128 devices in a mesh: tm: 16 (over x, y), tile: 8 (over z, core).
Axes of the slice: x: 4, y: 4, z: 4, core: 2. Of those that a mesh axis runs over, the one named last changes fastest.
Arguments:
- observed: float32 [9, 64, 8192], P(None, 'tile', 'tm'), may hold values from -6 to 6
- increments: float32 [9, 64, 8192], P(None, 'tile', 'tm'), may hold values from -0.15625 to 0.15625
- model: float32 [512, 256], P(('tm', 'tile')), may hold values from -6 to 6
- kernel: bfloat16 [256, 4, 9, 256, 256], P(('tm', 'tile')), may hold values from -0.1875 to 0.1875
- tile_index: int32 [256, 4], P(('tm', 'tile')), may hold values from 0 to 511, all different within a row
- station_of: int32 [64, 8192], P('tile', 'tm'), may hold values from 0 to 65535, as said below
- line_length: int32 [64], P('tile'), may hold values from 2048 to 8192, as said below
Outputs:
- grad_model: float32 [512, 256], P(('tm', 'tile'))
- grad_increments: float32 [9, 64, 8192], P(None, 'tile', 'tm')
Inputs may be any that keep to these rules, and one draw needn't show every extreme that they name: `station_of`: in the samples of one index pair of tile and tm (its block of lines and block of time), no station tile (value // 256) holds more than 32 samples, and one holds exactly 32. `line_length`: some line has all 8192 samples. `tile_index`: each row names 4 different cell tiles, and every cell tile is named by some row.
All inputs are finite; a program needn't handle non-finite values.
Results may differ from a plain program's by a relative error of at most 0.0031.
Values may be sent and summed in bfloat16 or wider, within the bound.
A program may use at most 128 MiB of HBM per device.

v0:
```python
import math
import jax
import jax.numpy as jnp
from jax import lax
from jax.sharding import PartitionSpec as P


def prefix(part, axis, combine, identity, reverse):
    count = lax.axis_size(axis)
    place = lax.axis_index(axis)
    ahead = count - 1 - place if reverse else place
    gathered = lax.all_gather(part, axis)
    state = jnp.zeros_like(part) + jnp.asarray(identity, part.dtype)

    def one(turn, state):
        source = count - 1 - turn if reverse else turn
        return combine(state, lax.dynamic_index_in_dim(gathered, source, 0, False))

    return lax.fori_loop(0, ahead, one, state)


def running_sum(values, backward):
    components, line_count, step_count = values.shape
    block_size = 128
    pieces = values.reshape(components, line_count, step_count // block_size, block_size)
    rows_index = lax.broadcasted_iota(jnp.int32, (block_size, block_size), 0)
    cols_index = lax.broadcasted_iota(jnp.int32, (block_size, block_size), 1)
    if backward:
        triangle = (rows_index >= cols_index).astype(jnp.float32)
    else:
        triangle = (rows_index <= cols_index).astype(jnp.float32)
    within = jnp.matmul(pieces, triangle, precision=lax.Precision.HIGHEST)
    if backward:
        block_total = within[..., 0]
        offsets = jnp.flip(jnp.cumsum(jnp.flip(block_total, 2), axis=2), 2) - block_total
    else:
        block_total = within[..., -1]
        offsets = jnp.cumsum(block_total, axis=2) - block_total
    return (within + offsets[..., None]).reshape(values.shape)


def shards(observed, increments, model, kernel, tile_index, station_of, line_length):
    components, line_count, step_count = observed.shape
    tiles_here = kernel.shape[0]
    tile_width = kernel.shape[-1]
    time_devices = lax.axis_size("tm")
    device_count = time_devices * lax.axis_size("tile")
    station_count = tiles_here * device_count
    row_count = line_count * step_count
    capacity = 2 * row_count // station_count
    total_steps = step_count * time_devices
    line_total = line_count * lax.axis_size("tile")
    station_gain = 1.0 / math.sqrt(line_total * total_steps / (station_count * tile_width))
    own_index = lax.axis_index("tm")
    partial_walk = running_sum(increments, False)
    walk_totals = partial_walk[:, :, -1]
    earlier = prefix(walk_totals, "tm", jnp.add, jnp.zeros_like(walk_totals), False)
    drift_walk = partial_walk + earlier[:, :, None]
    positions = own_index * step_count + jnp.arange(step_count, dtype=jnp.int32)
    inside = positions[None, :] < line_length[:, None]
    offset = drift_walk - observed
    flat_station = station_of.reshape(row_count)
    flat_inside = inside.reshape(row_count)
    flat_offset = offset.reshape(components, row_count)
    whole_model = lax.all_gather(model.astype(jnp.bfloat16), ("tm", "tile"), axis=0, tiled=True)
    chosen = whole_model[tile_index]
    predicted = jnp.einsum("skcij,skj->csi", kernel, chosen, preferred_element_type=jnp.float32)
    tile_of_row = flat_station // tile_width
    inner_station = jnp.where(flat_inside, flat_station % tile_width, tile_width)
    ordering = jnp.argsort(tile_of_row, stable=True)
    sorted_tiles = tile_of_row[ordering]
    starts = jnp.searchsorted(sorted_tiles, jnp.arange(station_count, dtype=jnp.int32))
    placed = jnp.arange(row_count, dtype=jnp.int32) - starts[sorted_tiles]
    slot_sorted = sorted_tiles * capacity + placed
    slot_of_row = jnp.zeros((row_count,), jnp.int32).at[ordering].set(slot_sorted)
    outgoing = (
        jnp.zeros((components, station_count * capacity), jnp.float32)
        .at[:, slot_of_row]
        .set(flat_offset)
    )
    labels = (
        jnp.full((station_count * capacity,), tile_width, jnp.int32)
        .at[slot_of_row]
        .set(inner_station)
    )
    arrived, arrived_labels = (
        lax.all_to_all(
            outgoing.reshape(components, station_count, capacity),
            ("tm", "tile"),
            split_axis=1,
            concat_axis=2,
            tiled=True,
        ),
        lax.all_to_all(
            labels.reshape(1, station_count, capacity),
            ("tm", "tile"),
            split_axis=1,
            concat_axis=2,
            tiled=True,
        ),
    )
    occupied = arrived_labels < tile_width
    station_ids = jnp.arange(tile_width, dtype=jnp.int32)
    matches = (arrived_labels[0][:, :, None] == station_ids).astype(jnp.float32)
    picked = jnp.einsum("csi,sri->csr", predicted, matches, precision=lax.Precision.HIGHEST)
    answer = jnp.where(occupied, picked + arrived, 0.0)
    station_sums = jnp.einsum("csr,sri->csi", answer, matches, precision=lax.Precision.HIGHEST)
    station_half = (station_sums * station_gain).astype(jnp.bfloat16)
    returned = lax.all_to_all(
        answer.astype(jnp.bfloat16), ("tm", "tile"), split_axis=2, concat_axis=1, tiled=True
    ).astype(answer.dtype)
    residual = returned.reshape(components, station_count * capacity)[:, slot_of_row]
    contributions = jnp.einsum(
        "skcij,csi->skj", kernel, station_half, preferred_element_type=jnp.float32
    )
    cell_total = model.shape[0] * device_count
    local_grad = (
        jnp.zeros((cell_total, tile_width), jnp.float32)
        .at[tile_index.reshape(-1)]
        .add(contributions.reshape(-1, tile_width))
    )
    grad_model = lax.psum_scatter(local_grad, ("tm", "tile"), scatter_dimension=0, tiled=True)
    residual_block = residual.reshape(components, line_count, step_count)
    partial_tail = running_sum(residual_block, True)
    tail_totals = partial_tail[:, :, 0]
    remaining = prefix(tail_totals, "tm", jnp.add, jnp.zeros_like(tail_totals), True)
    grad_increments = (partial_tail + remaining[:, :, None]) / math.sqrt(total_steps)
    return (grad_model, grad_increments)


def solution(mesh):
    in_specs = (
        P(None, "tile", "tm"),
        P(None, "tile", "tm"),
        P(("tm", "tile"), None),
        P(("tm", "tile"), None, None, None, None),
        P(("tm", "tile"), None),
        P("tile", "tm"),
        P("tile"),
    )
    out_specs = (P(("tm", "tile"), None), P(None, "tile", "tm"))
    return jax.shard_map(shards, mesh=mesh, in_specs=in_specs, out_specs=out_specs, check_vma=False)
```

profile of v0, /device:TPU:1, one launch (start us, length us, event | category | flops | bytes accessed | tf_op | source)
XLA Modules:
  0.0 415.5 jit_solution(10348112344737669025)
XLA Ops:
  8.7 5.8 %sort.17 = (s32[4096]{0:T(1024)}, s32[4096]{0:T(1024)S(1)}) sort(s32[4096]{0:T(1024)S(1)} %get-tuple-element.237, s32[4096]{0:T(1024)S(1)} %iota.37), dimensions={0}, to_apply=%region_0.0 | sort | flops 49152 | bytes 65536 | tf_op jit(solution)/shard_map/jit(argsort)/sort | solution.py:70
  14.5 23.0 %gather_fusion.1 = s32[4096]{0:T(1024)S(1)} fusion(s32[4096]{0:T(1024)S(1)} %get-tuple-element.237, s32[4096]{0:T(1024)S(1)} %get-tuple-element.238), kind=kCustom, calls=%fused_computation.1 | custom fusion | bytes 49152 | tf_op jit(solution)/shard_map/gather | solution.py:71
  37.6 23.3 %while.48 = (s32[]{:T(128)}, u32[256]{0:T(256)S(1)}, u32[256]{0:T(256)S(1)}, s32[4096]{0:T(1024)S(1)}, s32[]{:T(128)}, /*index=5*/s32[]{:T(128)}, s32[]{}) while((s32[]{:T(128)}, u32[256]{0:T(256)S(1)}, u32[256]{0:T(256)S(1)}, s32[4096]{0:T(1024)S(1)}, s32[]{:T(128)}, /*index=5*/s32[]{:T(128)}, s32[]{}) %tuple.85), condition=%wide.region_2.3_spmd.clone, body=%wide.region_1.2_spmd.clone.sunk | while | flops 4356 | bytes 16484 | solution.py:72
  37.6 1.7 gather_fusion
  39.4 1.7 gather_fusion
  41.2 1.7 gather_fusion
  43.0 1.7 gather_fusion
  48.4 1.7 gather_fusion
  53.8 1.7 gather_fusion
  59.1 1.7 gather_fusion
  60.9 25.7 %gather_fusion.2 = s32[4096]{0:T(1024)S(1)} fusion(s32[256]{0:T(256)S(1)} %convert_element_type.26, s32[4096]{0:T(1024)S(1)} %broadcast_clamp_fusion.1), kind=kCustom, calls=%fused_computation.2 | custom fusion | bytes 49152 | tf_op jit(solution)/shard_map/gather | solution.py:73
  86.7 15.5 %scatter_custom_fusion = s32[4096]{0:T(1024)S(1)} fusion(s32[4096]{0:T(1024)S(1)} %get-tuple-element.239, s32[4096]{0:T(1024)S(1)} %subtract_add_fusion, s32[]{:T(128)} %constant.112.clone.1), kind=kCustom, calls=%fused_computation.77 | custom fusion | bytes 16388 | tf_op jit(solution)/shard_map/scatter | solution.py:75
  102.3 15.5 %scatter_custom_fusion.1 = s32[8192]{0:T(1024)S(1)} fusion(s32[4096]{0:T(1024)S(1)} %get-tuple-element.235, s32[4096]{0:T(1024)S(1)} %get-tuple-element.236, s32[]{:T(128)} %constant.114.clone.1), kind=kCustom, calls=%fused_computation.67 | custom fusion | bytes 32772 | tf_op jit(solution)/shard_map/scatter | solution.py:84
  118.6 11.5 %all-to-all-start = ((s32[1,256,32]{2,0,1:T(1,128)}), s32[1,256,32]{2,0,1:T(1,128)S(1)}, u32[]{:S(2)}, u32[]{:S(2)}) async-start(s32[1,256,32]{2,0,1:T(1,128)} %bitcast.5), calls=%async_computation | async-start | bytes 262144 | tf_op jit(solution)/shard_map/all_to_all | solution.py:94
  132.0 18.4 %all-gather = f32[144,8,1]{1,2,0:T(1,128)S(1)} all-gather(f32[9,8,1]{1,2,0:T(1,128)S(1)} %copy.94), channel_id=2, replica_groups=mesh['tm'=16,'tile'=8] {'tm'}, dimensions={0}, use_global_device_ids=true | all-gather | bytes 4896 | tf_op jit(solution)/shard_map/all_gather | solution.py:12
  150.6 42.2 %all-gather.2 = bf16[128,4,256]{2,1,0:T(4,128)(2,1)S(1)} all-gather(bf16[1,4,256]{2,1,0:T(4,128)(2,1)S(1)} %convert_bitcast_fusion), channel_id=1, replica_groups=mesh['tm'=16,'tile'=8] {'tm','tile'}, dimensions={0}, use_global_device_ids=true | all-gather | bytes 264192 | tf_op jit(solution)/shard_map/all_gather | solution.py:65
  193.7 6.2 %convolution_bitcast_fusion.1 = f32[2,1,9,256,1]{3,1,4,2,0:T(1,128)S(1)} fusion(bf16[2,4,9,256,256]{4,3,2,1,0:T(8,128)(2,1)} %param.16, bf16[2,4,256,1,1]{2,3,1,4,0:T(2,128)(2,1)S(1)} %reshape.204), kind=kOutput, calls=%fused_computation.30 | convolution fusion | flops 9437184 | bytes 9459712 | tf_op jit(solution)/shard_map/skcij,skj->csi/dot_general | solution.py:67
  200.6 12.8 %scatter_custom_fusion.2 = f32[9,8192]{0,1:T(8,128)} fusion(s32[4096]{0:T(1024)S(1)} %get-tuple-element.235, f32[4096,9]{1,0:T(8,128)S(1)} %bitcast.115, f32[]{:T(128)} %constant.111.clone.1), kind=kCustom, calls=%fused_computation.24 | custom fusion | bytes 294916 | tf_op jit(solution)/shard_map/scatter | solution.py:79
  213.3 3.3 copy.99
  218.1 4.7 %all-to-all-start.1 = ((f32[128,1,576]{2,1,0:T(1,128)}), f32[128,1,576]{2,1,0:T(1,128)S(1)}, u32[]{:S(2)}, u32[]{:S(2)}) async-start(f32[128,1,576]{2,1,0:T(1,128)} %reshape.213), calls=%async_computation.1 | async-start | bytes 655360 | tf_op jit(solution)/shard_map/all_to_all | solution.py:87
  222.9 3.9 fusion.5
  226.8 7.5 %all-to-all-done.1 = f32[128,1,576]{2,1,0:T(1,128)S(1)} async-done(((f32[128,1,576]{2,1,0:T(1,128)}), f32[128,1,576]{2,1,0:T(1,128)S(1)}, u32[]{:S(2)}, u32[]{:S(2)}) %all-to-all-start.1) | async-done | bytes 294944 | tf_op jit(solution)/shard_map/all_to_all | solution.py:87
  238.3 2.8 copy.103
  241.2 4.8 %reshape.215 = bf16[128,2,288]{2,1,0:T(2,128)(2,1)} reshape(bf16[4096,2,9]{2,1,0:T(2,128)(2,1)S(1)} %bitcast.110) | data formatting | bytes 294912
  246.0 4.7 %all-to-all-start.2 = ((bf16[128,2,288]{2,1,0:T(2,128)(2,1)}), bf16[128,2,288]{2,1,0:T(2,128)(2,1)S(1)}, u32[]{:S(2)}, u32[]{:S(2)}) async-start(bf16[128,2,288]{2,1,0:T(2,128)(2,1)} %reshape.215), calls=%async_computation.2 | async-start | bytes 393216 | tf_op jit(solution)/shard_map/all_to_all | solution.py:109
  250.9 3.0 fusion.12
  253.9 5.0 %fusion.26 = f32[2,1,4,256,1]{3,1,4,2,0:T(1,128)S(1)} fusion(bf16[2,4,9,256,256]{4,3,2,1,0:T(8,128)(2,1)} %param.16, bf16[9,2,256,1,1]{2,0,1,3,4:T(8,128)(2,1)S(1)} %fusion.12), kind=kOutput, calls=%fused_computation.60 | convolution fusion | flops 9437184 | bytes 9454592 | tf_op jit(solution)/shard_map/skcij,csi->skj/dot_general | solution.py:113
  260.9 4.9 %reshape.216 = bf16[4096,2,9]{2,1,0:T(2,128)(2,1)S(1)} reshape(bf16[128,2,288]{2,1,0:T(2,128)(2,1)S(1)} %all-to-all-done.2) | data formatting | bytes 294912
  265.8 1.9 copy.124
  267.7 12.9 %gather_fusion.4 = bf16[4096,9]{1,0:T(8,128)(2,1)S(1)} fusion(bf16[9,8192]{0,1:T(8,128)(2,1)} %bitcast.113, s32[4096]{0:T(1024)S(1)} %get-tuple-element.234), kind=kCustom, calls=%fused_computation.4 | custom fusion | bytes 163840 | tf_op jit(solution)/shard_map/gather | solution.py:112
  281.9 18.6 %all-gather.1 = f32[144,8,1]{1,2,0:T(1,128)S(1)} all-gather(f32[9,8,1]{1,2,0:T(1,128)S(1)} %copy.110), channel_id=3, replica_groups=mesh['tm'=16,'tile'=8] {'tm'}, dimensions={0}, use_global_device_ids=true | all-gather | bytes 4896 | tf_op jit(solution)/shard_map/all_gather | solution.py:12
  302.4 105.0 %all-reduce.3.cloned.1.call-done = f32[512,256]{1,0:T(8,128)} async-done(((f32[512,256]{1,0:T(8,128)}), f32[512,256]{1,0:T(8,128)}) %all-reduce.3.cloned.1.call-update) | async-done | bytes 524304
  (157 shorter events, 29.1 us)
Async XLA Ops:
  7.2 123.0 %copy-start = (f32[9,8,512]{2,1,0:T(8,128)S(1)}, f32[9,8,512]{2,1,0:T(8,128)}, u32[]{:S(2)}) copy-start(f32[9,8,512]{2,1,0:T(8,128)} %param.14) | copy-start | bytes 442372
  60.9 69.2 %copy-start.3 = (s32[2,4]{1,0:T(2,128)S(1)}, s32[2,4]{1,0:T(2,128)}, u32[]{:S(2)}) copy-start(s32[2,4]{1,0:T(2,128)} %param.17) | copy-start | bytes 100
  60.9 89.7 %copy-start.2 = (f32[4,256]{1,0:T(4,128)S(1)}, f32[4,256]{1,0:T(4,128)}, u32[]{:S(2)}) copy-start(f32[4,256]{1,0:T(4,128)} %param.15) | copy-start | bytes 12292
  86.7 106.9 %copy-start.1 = (f32[9,8,512]{2,1,0:T(8,128)S(1)}, f32[9,8,512]{2,1,0:T(8,128)}, u32[]{:S(2)}) copy-start(f32[9,8,512]{2,1,0:T(8,128)} %param.13) | copy-start | bytes 442372
  118.6 99.5 %all-to-all-start = ((s32[1,256,32]{2,0,1:T(1,128)}), s32[1,256,32]{2,0,1:T(1,128)S(1)}, u32[]{:S(2)}, u32[]{:S(2)}) async-start(s32[1,256,32]{2,0,1:T(1,128)} %bitcast.5), calls=%async_computation | async-start | bytes 262144 | tf_op jit(solution)/shard_map/all_to_all | solution.py:94
  218.1 16.2 %all-to-all-start.1 = ((f32[128,1,576]{2,1,0:T(1,128)}), f32[128,1,576]{2,1,0:T(1,128)S(1)}, u32[]{:S(2)}, u32[]{:S(2)}) async-start(f32[128,1,576]{2,1,0:T(1,128)} %reshape.213), calls=%async_computation.1 | async-start | bytes 655360 | tf_op jit(solution)/shard_map/all_to_all | solution.py:87
  246.0 15.0 %all-to-all-start.2 = ((bf16[128,2,288]{2,1,0:T(2,128)(2,1)}), bf16[128,2,288]{2,1,0:T(2,128)(2,1)S(1)}, u32[]{:S(2)}, u32[]{:S(2)}) async-start(bf16[128,2,288]{2,1,0:T(2,128)(2,1)} %reshape.215), calls=%async_computation.2 | async-start | bytes 393216 | tf_op jit(solution)/shard_map/all_to_all | solution.py:109
  250.6 156.8 %all-reduce.3.cloned.1.call-start = ((), (), s32[]{:S(2)}) async-start(), calls=%async_computation.3 | async-start | bytes 1048576
Sparse Core Ops, SparseCore 0:
  260.5 146.8 all-reduce.2
where the time goes:
time: 416 us
  local copies, waits for them, and re-layouts  155 us (37%)
  waiting for transfers between devices  113 us (27%)
  blocking collectives  79.2 us (19%)
  starting transfers between devices  21.1 us (5%)
  matrix products  18.8 us (5%)
  between operations  14.5 us (3%)
  other arithmetic  12.3 us (3%)
    unnamed x2, waiting for transfers between devices  105 us
    all_gather x1, blocking collectives, shards(): lax.all_gather(model.astype(jnp.bfloat16), ('tm', 'tile'), axis=0, tiled=...  42.2 us
    all_gather x2, blocking collectives, prefix(): gathered = lax.all_gather(part, axis)  37 us
    gather x1, local copies, waits for them, and re-layouts, shards(): placed = jnp.arange(row_count, dtype=jnp.int32) - starts[sorted_tiles]  25.7 us
    gather x1, local copies, waits for them, and re-layouts, shards(): sorted_tiles = tile_of_row[ordering]  23 us
    gather x13, local copies, waits for them, and re-layouts, shards(): jnp.searchsorted(sorted_tiles, jnp.arange(station_count, dtype=jnp.int32))  22.4 us
    scatter x1, local copies, waits for them, and re-layouts, shards(): labels = jnp.full((station_count * capacity,), tile_width, jnp.int32).at[...  15.5 us
    scatter x1, local copies, waits for them, and re-layouts, shards(): jnp.zeros((row_count,), jnp.int32).at[ordering].set(slot_sorted)  15.5 us
  transfers between devices with their start and end apart: 4, of which 3 were waited for; matrix products, arithmetic and copies ran while one was open for 15% of the time, Pallas kernels for 0%

commit v1 on v0

--- a/solution.py
+++ b/solution.py
@@ -3,6 +3,11 @@
 import jax.numpy as jnp
 from jax import lax
 from jax.sharding import PartitionSpec as P
+
+
+def swapped_in(shard, name, dim):
+    stack = jnp.stack([shard] * lax.axis_size(name))
+    return jnp.concatenate(lax.all_to_all(stack, name, 0, 0), axis=dim)
 
 
 def prefix(part, axis, combine, identity, reverse):
@@ -62,7 +67,7 @@
     flat_station = station_of.reshape(row_count)
     flat_inside = inside.reshape(row_count)
     flat_offset = offset.reshape(components, row_count)
-    whole_model = lax.all_gather(model.astype(jnp.bfloat16), ("tm", "tile"), axis=0, tiled=True)
+    whole_model = swapped_in(model.astype(jnp.bfloat16), ("tm", "tile"), 0)
     chosen = whole_model[tile_index]
     predicted = jnp.einsum("skcij,skj->csi", kernel, chosen, preferred_element_type=jnp.float32)
     tile_of_row = flat_station // tile_width

time: 416 us -> 396 us (0.952)
  blocking collectives: 79.2 us -> 36.8 us
  starting transfers between devices: 21.1 us -> 38.9 us
    all_gather x1 -> x0, blocking collectives: 42.2 us -> none  [shards(): lax.all_gather(model.astype(jnp.bfloat16), ('tm', 'tile'), axis=0, tiled=...]
    all_to_all x0 -> x1, starting transfers between devices: none -> 13.7 us  [swapped_in(): return jnp.concatenate(lax.all_to_all(stack, name, 0, 0), axis=dim)]
    all_to_all x0 -> x1, waiting for transfers between devices: none -> 10.8 us  [swapped_in(): return jnp.concatenate(lax.all_to_all(stack, name, 0, 0), axis=dim)]
    all_to_all x1, waiting for transfers between devices: 7.51 us -> 0.96 us  [shards(): lax.all_to_all(outgoing.reshape(components, station_count, capacity), ('t...]
    all_to_all x1, starting transfers between devices: 4.65 us -> 8.96 us  [shards(): lax.all_to_all(answer.astype(jnp.bfloat16), ('tm', 'tile'), split_axis=2,...]
    unnamed x16 -> x15, local copies, waits for them, and re-layouts: 13.8 us -> 13.7 us
  transfers between devices with their start and end apart: 4 -> 5, of which waited for: 3 -> 4; matrix products, arithmetic and copies ran while one was open for 15% -> 16% of each run, Pallas kernels for 0% -> 0%
where the time goes in v1:
time: 396 us
  local copies, waits for them, and re-layouts  156 us (39%)
  waiting for transfers between devices  117 us (30%)
  starting transfers between devices  38.9 us (10%)
  blocking collectives  36.8 us (9%)
  matrix products  18.8 us (5%)
  between operations  14.5 us (4%)
  other arithmetic  12.3 us (3%)
    unnamed x2, waiting for transfers between devices  105 us
    all_gather x2, blocking collectives, prefix(): gathered = lax.all_gather(part, axis)  36.8 us
    gather x1, local copies, waits for them, and re-layouts, shards(): placed = jnp.arange(row_count, dtype=jnp.int32) - starts[sorted_tiles]  25.7 us
    gather x1, local copies, waits for them, and re-layouts, shards(): sorted_tiles = tile_of_row[ordering]  23 us
    gather x13, local copies, waits for them, and re-layouts, shards(): jnp.searchsorted(sorted_tiles, jnp.arange(station_count, dtype=jnp.int32))  22.4 us
    scatter x1, local copies, waits for them, and re-layouts, shards(): labels = jnp.full((station_count * capacity,), tile_width, jnp.int32).at[...  15.5 us
    scatter x1, local copies, waits for them, and re-layouts, shards(): jnp.zeros((row_count,), jnp.int32).at[ordering].set(slot_sorted)  15.5 us
    all_to_all x1, starting transfers between devices, swapped_in(): return jnp.concatenate(lax.all_to_all(stack, name, 0, 0), axis=dim)  13.7 us
  transfers between devices with their start and end apart: 5, of which 4 were waited for; matrix products, arithmetic and copies ran while one was open for 16% of the time, Pallas kernels for 0%

profile of v1, /device:TPU:1, one launch (start us, length us, event | category | flops | bytes accessed | tf_op | source)
XLA Modules:
  0.0 396.0 jit_solution(16673762703003015741)
XLA Ops:
  8.7 5.8 %sort.17 = (s32[4096]{0:T(1024)}, s32[4096]{0:T(1024)S(1)}) sort(s32[4096]{0:T(1024)S(1)} %get-tuple-element.237, s32[4096]{0:T(1024)S(1)} %iota.37), dimensions={0}, to_apply=%region_0.0 | sort | flops 49152 | bytes 65536 | tf_op jit(solution)/shard_map/jit(argsort)/sort | solution.py:75
  14.5 23.0 %gather_fusion.1 = s32[4096]{0:T(1024)S(1)} fusion(s32[4096]{0:T(1024)S(1)} %get-tuple-element.237, s32[4096]{0:T(1024)S(1)} %get-tuple-element.238), kind=kCustom, calls=%fused_computation.1 | custom fusion | bytes 49152 | tf_op jit(solution)/shard_map/gather | solution.py:76
  37.6 23.3 %while.48 = (s32[]{:T(128)}, u32[256]{0:T(256)S(1)}, u32[256]{0:T(256)S(1)}, s32[4096]{0:T(1024)S(1)}, s32[]{:T(128)}, /*index=5*/s32[]{:T(128)}, s32[]{}) while((s32[]{:T(128)}, u32[256]{0:T(256)S(1)}, u32[256]{0:T(256)S(1)}, s32[4096]{0:T(1024)S(1)}, s32[]{:T(128)}, /*index=5*/s32[]{:T(128)}, s32[]{}) %tuple.85), condition=%wide.region_2.3_spmd.clone, body=%wide.region_1.2_spmd.clone.sunk | while | flops 4356 | bytes 16484 | solution.py:77
  37.6 1.7 gather_fusion
  39.4 1.7 gather_fusion
  41.2 1.7 gather_fusion
  43.0 1.7 gather_fusion
  48.4 1.7 gather_fusion
  53.8 1.7 gather_fusion
  59.1 1.7 gather_fusion
  60.9 25.7 %gather_fusion.2 = s32[4096]{0:T(1024)S(1)} fusion(s32[256]{0:T(256)S(1)} %convert_element_type.26, s32[4096]{0:T(1024)S(1)} %broadcast_clamp_fusion.1), kind=kCustom, calls=%fused_computation.2 | custom fusion | bytes 49152 | tf_op jit(solution)/shard_map/gather | solution.py:78
  86.7 15.5 %scatter_custom_fusion = s32[4096]{0:T(1024)S(1)} fusion(s32[4096]{0:T(1024)S(1)} %get-tuple-element.239, s32[4096]{0:T(1024)S(1)} %subtract_add_fusion, s32[]{:T(128)} %constant.112.clone.1), kind=kCustom, calls=%fused_computation.77 | custom fusion | bytes 16388 | tf_op jit(solution)/shard_map/scatter | solution.py:80
  102.2 15.5 %scatter_custom_fusion.1 = s32[8192]{0:T(1024)S(1)} fusion(s32[4096]{0:T(1024)S(1)} %get-tuple-element.235, s32[4096]{0:T(1024)S(1)} %get-tuple-element.236, s32[]{:T(128)} %constant.114.clone.1), kind=kCustom, calls=%fused_computation.67 | custom fusion | bytes 32772 | tf_op jit(solution)/shard_map/scatter | solution.py:89
  118.6 11.5 %all-to-all-start = ((s32[1,256,32]{2,0,1:T(1,128)}), s32[1,256,32]{2,0,1:T(1,128)S(1)}, u32[]{:S(2)}, u32[]{:S(2)}) async-start(s32[1,256,32]{2,0,1:T(1,128)} %bitcast.5), calls=%async_computation | async-start | bytes 262144 | tf_op jit(solution)/shard_map/all_to_all | solution.py:99
  132.0 18.4 %all-gather = f32[144,8,1]{1,2,0:T(1,128)S(1)} all-gather(f32[9,8,1]{1,2,0:T(1,128)S(1)} %copy.94), channel_id=2, replica_groups=mesh['tm'=16,'tile'=8] {'tm'}, dimensions={0}, use_global_device_ids=true | all-gather | bytes 4896 | tf_op jit(solution)/shard_map/all_gather | solution.py:17
  151.5 12.8 %scatter_custom_fusion.2 = f32[9,8192]{0,1:T(8,128)} fusion(s32[4096]{0:T(1024)S(1)} %get-tuple-element.235, f32[4096,9]{1,0:T(8,128)S(1)} %bitcast.113, f32[]{:T(128)} %constant.111.clone.1), kind=kCustom, calls=%fused_computation.24 | custom fusion | bytes 294916 | tf_op jit(solution)/shard_map/scatter | solution.py:84
  164.2 3.3 copy.99
  169.7 13.7 %all-to-all-start.1 = ((bf16[128,4,256]{2,1,0:T(4,128)(2,1)}), bf16[128,4,256]{2,1,0:T(4,128)(2,1)S(1)}, u32[]{:S(2)}, u32[]{:S(2)}) async-start(bf16[128,4,256]{2,1,0:T(4,128)(2,1)} %stack.2), calls=%async_computation.1 | async-start | bytes 524288 | tf_op jit(solution)/shard_map/all_to_all | solution.py:10
  183.6 10.8 %all-to-all-done.1 = bf16[128,4,256]{2,1,0:T(4,128)(2,1)S(1)} async-done(((bf16[128,4,256]{2,1,0:T(4,128)(2,1)}), bf16[128,4,256]{2,1,0:T(4,128)(2,1)S(1)}, u32[]{:S(2)}, u32[]{:S(2)}) %all-to-all-start.1) | async-done | bytes 262176 | tf_op jit(solution)/shard_map/all_to_all | solution.py:10
  194.4 4.7 %all-to-all-start.2 = ((f32[128,1,576]{2,1,0:T(1,128)}), f32[128,1,576]{2,1,0:T(1,128)S(1)}, u32[]{:S(2)}, u32[]{:S(2)}) async-start(f32[128,1,576]{2,1,0:T(1,128)} %reshape.217), calls=%async_computation.2 | async-start | bytes 655360 | tf_op jit(solution)/shard_map/all_to_all | solution.py:92
  199.7 6.2 %convolution_bitcast_fusion.1 = f32[2,1,9,256,1]{3,1,4,2,0:T(1,128)S(1)} fusion(bf16[2,4,9,256,256]{4,3,2,1,0:T(8,128)(2,1)} %param.16, bf16[2,4,256,1,1]{2,3,1,4,0:T(2,128)(2,1)S(1)} %reshape.208), kind=kOutput, calls=%fused_computation.30 | convolution fusion | flops 9437184 | bytes 9459712 | tf_op jit(solution)/shard_map/skcij,skj->csi/dot_general | solution.py:72
  205.9 3.9 fusion.5
  214.8 2.8 copy.103
  217.6 4.7 %reshape.219 = bf16[128,2,288]{2,1,0:T(2,128)(2,1)} reshape(bf16[4096,2,9]{2,1,0:T(2,128)(2,1)S(1)} %bitcast.108) | data formatting | bytes 294912
  222.4 9.0 %all-to-all-start.3 = ((bf16[128,2,288]{2,1,0:T(2,128)(2,1)}), bf16[128,2,288]{2,1,0:T(2,128)(2,1)S(1)}, u32[]{:S(2)}, u32[]{:S(2)}) async-start(bf16[128,2,288]{2,1,0:T(2,128)(2,1)} %reshape.219), calls=%async_computation.3 | async-start | bytes 393216 | tf_op jit(solution)/shard_map/all_to_all | solution.py:114
  231.4 3.0 fusion.12
  234.4 5.0 %fusion.26 = f32[2,1,4,256,1]{3,1,4,2,0:T(1,128)S(1)} fusion(bf16[2,4,9,256,256]{4,3,2,1,0:T(8,128)(2,1)} %param.16, bf16[9,2,256,1,1]{2,0,1,3,4:T(8,128)(2,1)S(1)} %fusion.12), kind=kOutput, calls=%fused_computation.60 | convolution fusion | flops 9437184 | bytes 9454592 | tf_op jit(solution)/shard_map/skcij,csi->skj/dot_general | solution.py:118
  241.6 4.9 %reshape.220 = bf16[4096,2,9]{2,1,0:T(2,128)(2,1)S(1)} reshape(bf16[128,2,288]{2,1,0:T(2,128)(2,1)S(1)} %all-to-all-done.3) | data formatting | bytes 294912
  246.5 1.9 copy.124
  248.4 12.9 %gather_fusion.4 = bf16[4096,9]{1,0:T(8,128)(2,1)S(1)} fusion(bf16[9,8192]{0,1:T(8,128)(2,1)} %bitcast.111, s32[4096]{0:T(1024)S(1)} %get-tuple-element.234), kind=kCustom, calls=%fused_computation.4 | custom fusion | bytes 163840 | tf_op jit(solution)/shard_map/gather | solution.py:117
  262.5 18.4 %all-gather.1 = f32[144,8,1]{1,2,0:T(1,128)S(1)} all-gather(f32[9,8,1]{1,2,0:T(1,128)S(1)} %copy.110), channel_id=3, replica_groups=mesh['tm'=16,'tile'=8] {'tm'}, dimensions={0}, use_global_device_ids=true | all-gather | bytes 4896 | tf_op jit(solution)/shard_map/all_gather | solution.py:17
  282.8 105.0 %all-reduce.3.cloned.1.call-done = f32[512,256]{1,0:T(8,128)} async-done(((f32[512,256]{1,0:T(8,128)}), f32[512,256]{1,0:T(8,128)}) %all-reduce.3.cloned.1.call-update) | async-done | bytes 524304
  (159 shorter events, 30.8 us)
Async XLA Ops:
  7.2 123.0 %copy-start = (f32[9,8,512]{2,1,0:T(8,128)S(1)}, f32[9,8,512]{2,1,0:T(8,128)}, u32[]{:S(2)}) copy-start(f32[9,8,512]{2,1,0:T(8,128)} %param.14) | copy-start | bytes 442372
  60.9 69.2 %copy-start.3 = (s32[2,4]{1,0:T(2,128)S(1)}, s32[2,4]{1,0:T(2,128)}, u32[]{:S(2)}) copy-start(s32[2,4]{1,0:T(2,128)} %param.17) | copy-start | bytes 100
  60.9 89.8 %copy-start.1 = (f32[9,8,512]{2,1,0:T(8,128)S(1)}, f32[9,8,512]{2,1,0:T(8,128)}, u32[]{:S(2)}) copy-start(f32[9,8,512]{2,1,0:T(8,128)} %param.13) | copy-start | bytes 442372
  118.6 50.4 %all-to-all-start = ((s32[1,256,32]{2,0,1:T(1,128)}), s32[1,256,32]{2,0,1:T(1,128)S(1)}, u32[]{:S(2)}, u32[]{:S(2)}) async-start(s32[1,256,32]{2,0,1:T(1,128)} %bitcast.5), calls=%async_computation | async-start | bytes 262144 | tf_op jit(solution)/shard_map/all_to_all | solution.py:99
  164.2 4.8 %copy-start.2 = (f32[4,256]{1,0:T(4,128)S(1)}, f32[4,256]{1,0:T(4,128)}, u32[]{:S(2)}) copy-start(f32[4,256]{1,0:T(4,128)} %param.15) | copy-start | bytes 12292
  169.7 24.6 %all-to-all-start.1 = ((bf16[128,4,256]{2,1,0:T(4,128)(2,1)}), bf16[128,4,256]{2,1,0:T(4,128)(2,1)S(1)}, u32[]{:S(2)}, u32[]{:S(2)}) async-start(bf16[128,4,256]{2,1,0:T(4,128)(2,1)} %stack.2), calls=%async_computation.1 | async-start | bytes 524288 | tf_op jit(solution)/shard_map/all_to_all | solution.py:10
  194.4 16.4 %all-to-all-start.2 = ((f32[128,1,576]{2,1,0:T(1,128)}), f32[128,1,576]{2,1,0:T(1,128)S(1)}, u32[]{:S(2)}, u32[]{:S(2)}) async-start(f32[128,1,576]{2,1,0:T(1,128)} %reshape.217), calls=%async_computation.2 | async-start | bytes 655360 | tf_op jit(solution)/shard_map/all_to_all | solution.py:92
  222.4 19.2 %all-to-all-start.3 = ((bf16[128,2,288]{2,1,0:T(2,128)(2,1)}), bf16[128,2,288]{2,1,0:T(2,128)(2,1)S(1)}, u32[]{:S(2)}, u32[]{:S(2)}) async-start(bf16[128,2,288]{2,1,0:T(2,128)(2,1)} %reshape.219), calls=%async_computation.3 | async-start | bytes 393216 | tf_op jit(solution)/shard_map/all_to_all | solution.py:114
  231.3 156.5 %all-reduce.3.cloned.1.call-start = ((), (), s32[]{:S(2)}) async-start(), calls=%async_computation.4 | async-start | bytes 1048576
Sparse Core Ops, SparseCore 0:
  241.0 146.7 all-reduce.2
